TPU v7x, 512 devices: a whole 4x8x8 slice. The times are simulated.
512 devices in a mesh: lang: 64 (over y, z), rep: 8 (over x, core).
Axes of the slice: x: 4, y: 8, z: 8, core: 2. Of those that a mesh axis runs over, the one named last changes fastest.
Arguments:
- tokens: bfloat16 [65536, 1024], P(('lang', 'rep')), may hold values from -24 to 24
- grad_out: bfloat16 [65536, 1024], P(('lang', 'rep')), may hold values from -24 to 24
- lang_ids: int32 [65536], P(('lang', 'rep')), may hold values from 0 to 7, as said below
- slot_ids: int32 [65536], P(('lang', 'rep')), may hold values from 0 to 23, as said below
- w_up: bfloat16 [1024, 32768], P(None, 'lang'), may hold values from -0.1875 to 0.1875
- w_down_t: bfloat16 [1024, 32768], P(None, 'lang'), may hold values from -0.09375 to 0.09375
Outputs:
- ffn_out: bfloat16 [65536, 1024], P(('lang', 'rep'))
- grad_tokens: bfloat16 [65536, 1024], P(('lang', 'rep'))
- grad_up: float32 [1024, 32768], P('rep', 'lang')
- grad_down: float32 [1024, 32768], P('rep', 'lang')
Inputs may be any that keep to these rules, and one draw needn't show every extreme that they name: `lang_ids`: each device holds 128 consecutive tokens. On every device one language, the same on all devices, has exactly 24 tokens; every other language has at most 18 tokens on a device, and on every device one of them has exactly 18. `slot_ids`: on each device the tokens of one language hold the distinct slots 0 to their count minus 1, in no particular order.
All inputs are finite; a program needn't handle non-finite values.
Results may differ from a plain program's by a relative error of at most 0.0058.
Values may be sent and summed in bfloat16 or wider, within the bound.
A program may use at most 128 MiB of HBM per device.

v0:
```python
import jax
import jax.numpy as jnp
from jax import lax
from jax.sharding import Mesh
from jax.sharding import PartitionSpec as P

MODULES = 8
TOK_DEV = 128
CAPACITY = 18
INV_ROOT_TWO = 0.7071067811865476
INV_ROOT_TAU = 0.3989422804014327


def gelu_value(values):
    return 0.5 * values * (1.0 + lax.erf(values * INV_ROOT_TWO))


def gelu_slope(values):
    return (
        0.5 * (1.0 + lax.erf(values * INV_ROOT_TWO))
        + values * jnp.exp(-0.5 * values * values) * INV_ROOT_TAU
    )


def per_device(tokens, grad_out, lang_ids, slot_ids, w_up, w_down_t):
    feature_width = tokens.shape[1]
    capacity = CAPACITY
    keep_mask = slot_ids < capacity
    target = jnp.where(keep_mask, lang_ids * capacity + slot_ids, MODULES * capacity)
    safe_slot = jnp.minimum(slot_ids, capacity - 1)
    token_scale = 1.0 / TOK_DEV

    def place(values):
        buffer = (
            jnp.zeros((MODULES * capacity, feature_width), values.dtype)
            .at[target]
            .set(values, mode="drop")
        )
        return buffer.reshape(MODULES, capacity, feature_width)

    def dispatch(values):
        by_y = lax.all_to_all(place(values), "ly", split_axis=0, concat_axis=0, tiled=True)
        every = lax.all_gather(by_y, "lz", axis=0, tiled=True)
        return every.reshape(-1, feature_width)

    def give_back(rows):
        parts = rows.astype(jnp.float32).reshape(-1, capacity, feature_width)
        summed = lax.psum_scatter(parts, "lz", scatter_dimension=0, tiled=True)
        summed = summed.astype(jnp.bfloat16)
        return lax.all_to_all(summed, "ly", split_axis=0, concat_axis=0, tiled=True)

    def collect(returned):
        picked = returned[lang_ids, safe_slot]
        return jnp.where(keep_mask[:, None], picked, jnp.zeros_like(picked))

    flat_tokens = dispatch(tokens)
    flat_grads = dispatch(grad_out)
    pre_flat = jnp.dot(flat_tokens, w_up, preferred_element_type=jnp.float32)
    hidden_flat = gelu_value(pre_flat).astype(jnp.bfloat16)
    partial_rows = lax.dot_general(
        hidden_flat, w_down_t, (((1,), (1,)), ((), ())), preferred_element_type=jnp.float32
    ).astype(jnp.bfloat16)
    returned = give_back(partial_rows)
    grad_down = lax.psum_scatter(
        lax.dot_general(
            flat_grads, hidden_flat, (((0,), (0,)), ((), ())), preferred_element_type=jnp.float32
        )
        * token_scale,
        "rep",
        scatter_dimension=0,
        tiled=True,
    )
    d_hidden = jnp.dot(flat_grads, w_down_t, preferred_element_type=jnp.float32)
    d_pre = (d_hidden * gelu_slope(pre_flat)).astype(jnp.bfloat16)
    grad_up = lax.psum_scatter(
        lax.dot_general(
            flat_tokens, d_pre, (((0,), (0,)), ((), ())), preferred_element_type=jnp.float32
        )
        * token_scale,
        "rep",
        scatter_dimension=0,
        tiled=True,
    )
    dx_part = lax.dot_general(
        d_pre, w_up, (((1,), (1,)), ((), ())), preferred_element_type=jnp.float32
    ).astype(jnp.bfloat16)
    dx_back = give_back(dx_part)
    return (collect(returned), collect(dx_back), grad_up, grad_down)


def solution(mesh):
    n_lang = mesh.shape["lang"]
    groups = n_lang // MODULES
    devices = mesh.devices.reshape(MODULES, groups, mesh.shape["rep"])
    split_mesh = Mesh(devices, ("ly", "lz", "rep"))
    rows = P(("ly", "lz", "rep"), None)
    ids = P(("ly", "lz", "rep"))
    cols = P(None, ("ly", "lz"))
    return jax.shard_map(
        per_device,
        mesh=split_mesh,
        in_specs=(rows, rows, ids, ids, cols, cols),
        out_specs=(rows, rows, P("rep", ("ly", "lz")), P("rep", ("ly", "lz"))),
        check_vma=False,
    )
```

profile of v0, /device:TPU:8, one launch (start us, length us, event | category | flops | bytes accessed | tf_op | source)
XLA Modules:
  0.0 392.5 jit_solution(12223299433012391685)
XLA Ops:
  9.7 20.6 %all_to_all.20 = bf16[8,18,1024]{2,1,0:T(8,128)(2,1)S(1)} all-to-all(bf16[8,18,1024]{2,1,0:T(8,128)(2,1)S(1)} %reshape.37), channel_id=1, replica_groups=mesh['ly'=8,'lz'=8,'rep'=8] {'ly'}, dimensions={0} | all-to-all | bytes 589824 | tf_op jit(solution)/shard_map/all_to_all | solution.py:42
  33.0 15.6 %all_to_all.21 = bf16[8,18,1024]{2,1,0:T(8,128)(2,1)S(1)} all-to-all(bf16[8,18,1024]{2,1,0:T(8,128)(2,1)S(1)} %reshape.33), channel_id=1, replica_groups=mesh['ly'=8,'lz'=8,'rep'=8] {'ly'}, dimensions={0} | all-to-all | bytes 589824 | tf_op jit(solution)/shard_map/all_to_all | solution.py:42
  49.6 27.2 %all-gather.5.cloned.1.call-done = bf16[64,18,1024]{2,0,1:T(8,128)(2,1)} async-done(((bf16[8,18,1024]{2,0,1:T(8,128)(2,1)}), bf16[64,18,1024]{2,0,1:T(8,128)(2,1)}) %all-gather.5.cloned.1.call-update) | async-done | bytes 2359312 | tf_op jit(solution)/shard_map/all_gather | solution.py:43
  76.8 4.7 %copy.18 = bf16[64,18,1024]{2,1,0:T(8,128)(2,1)} copy(bf16[64,18,1024]{2,0,1:T(8,128)(2,1)} %all-gather.5.cloned.1.call-done) | data formatting | bytes 4718592 | tf_op jit(solution)/shard_map/all_gather | solution.py:43
  81.5 2.9 reshape.38
  84.4 37.9 %all-gather.3.cloned.1.call-done = bf16[64,18,1024]{2,0,1:T(8,128)(2,1)} async-done(((bf16[8,18,1024]{2,0,1:T(8,128)(2,1)}), bf16[64,18,1024]{2,0,1:T(8,128)(2,1)}) %all-gather.3.cloned.1.call-update) | async-done | bytes 2359312 | tf_op jit(solution)/shard_map/all_gather | solution.py:43
  122.3 4.7 %copy.15 = bf16[64,18,1024]{2,1,0:T(8,128)(2,1)} copy(bf16[64,18,1024]{2,0,1:T(8,128)(2,1)} %all-gather.3.cloned.1.call-done) | data formatting | bytes 4718592 | tf_op jit(solution)/shard_map/all_gather | solution.py:43
  127.0 4.3 %reshape.34 = bf16[1152,1024]{1,0:T(8,128)(2,1)} reshape(bf16[64,18,1024]{2,1,0:T(8,128)(2,1)} %copy.15) | data formatting | bytes 4718592 | tf_op jit(solution)/shard_map/reshape | solution.py:44
  131.4 4.4 %multiply_convert_fusion = (bf16[1152,512]{1,0:T(8,128)(2,1)}, f32[1152,512]{1,0:T(8,128)S(1)}) fusion(bf16[1152,1024]{1,0:T(8,128)(2,1)} %reshape.34, bf16[1024,512]{1,0:T(8,128)(2,1)S(1)} %copy-done), kind=kOutput, calls=%fused_computation.15 | convolution fusion | flops 1210908672 | bytes 6946816 | tf_op jit(solution)/shard_map/dot_general | solution.py:58
  135.7 2.0 fusion.2
  138.8 3.7 fusion.1
  142.4 5.6 %reshape.44 = f32[64,18,1024]{2,1,0:T(8,128)} reshape(f32[1152,1024]{1,0:T(8,128)} %fusion.1) | data formatting | bytes 9437184 | tf_op jit(solution)/shard_map/reshape | solution.py:47
  148.1 5.1 %fusion = f32[1152,1024]{1,0:T(8,128)} fusion(bf16[1152,512]{1,0:T(8,128)(2,1)} %get-tuple-element.8, bf16[1024,512]{1,0:T(8,128)(2,1)} %param.11), kind=kOutput, calls=%fused_computation.6 | convolution fusion | flops 1210318848 | bytes 6946816 | tf_op jit(solution)/shard_map/dot_general | solution.py:60
  153.2 5.6 %reshape.42 = f32[64,18,1024]{2,1,0:T(8,128)} reshape(f32[1152,1024]{1,0:T(8,128)} %fusion) | data formatting | bytes 9437184 | tf_op jit(solution)/shard_map/reshape | solution.py:47
  158.8 5.2 %convolution_multiply_fusion.2 = f32[1024,512]{1,0:T(8,128)} fusion(bf16[1152,1024]{1,0:T(8,128)(2,1)} %reshape.34, bf16[1152,512]{1,0:T(8,128)(2,1)} %copy-done.3), kind=kOutput, calls=%fused_computation.18 | convolution fusion | flops 1208483840 | bytes 5636096 | tf_op jit(solution)/shard_map/dot_general | solution.py:76
  164.3 4.1 %convolution_multiply_fusion.1 = f32[1024,512]{1,0:T(8,128)} fusion(bf16[1152,1024]{1,0:T(8,128)(2,1)S(1)} %reshape.38, bf16[1152,512]{1,0:T(8,128)(2,1)} %get-tuple-element.8), kind=kOutput, calls=%fused_computation.17 | convolution fusion | flops 1208483840 | bytes 5636096 | tf_op jit(solution)/shard_map/dot_general | solution.py:65
  168.5 56.3 %reduce-scatter.7.cloned.1.call-done = f32[8,18,1024]{2,1,0:T(8,128)} async-done(((f32[64,18,1024]{2,1,0:T(8,128)}), f32[8,18,1024]{2,1,0:T(8,128)}) %reduce-scatter.7.cloned.1.call-update) | async-done | bytes 589840 | tf_op jit(solution)/shard_map/reduce_scatter | solution.py:48
  224.8 1.9 convert_element_type.25
  226.7 7.3 %all-to-all-start.3 = ((bf16[8,18,1024]{2,1,0:T(8,128)(2,1)}), bf16[8,18,1024]{2,1,0:T(8,128)(2,1)S(1)}, u32[]{:S(2)}, u32[]{:S(2)}) async-start(bf16[8,18,1024]{2,1,0:T(8,128)(2,1)} %convert_element_type.25), calls=%async_computation.5 | async-start | bytes 786432 | tf_op jit(solution)/shard_map/all_to_all | solution.py:50
  234.0 70.2 %reduce-scatter.5.cloned.1.call-done = f32[8,18,1024]{2,1,0:T(8,128)} async-done(((f32[64,18,1024]{2,1,0:T(8,128)}), f32[8,18,1024]{2,1,0:T(8,128)}) %reduce-scatter.5.cloned.1.call-update) | async-done | bytes 589840 | tf_op jit(solution)/shard_map/reduce_scatter | solution.py:48
  306.1 7.3 %all-to-all-start.1 = ((bf16[8,18,1024]{2,1,0:T(8,128)(2,1)}), bf16[8,18,1024]{2,1,0:T(8,128)(2,1)S(1)}, u32[]{:S(2)}, u32[]{:S(2)}) async-start(bf16[8,18,1024]{2,1,0:T(8,128)(2,1)} %convert_element_type.22), calls=%async_computation.2 | async-start | bytes 786432 | tf_op jit(solution)/shard_map/all_to_all | solution.py:50
  315.2 11.5 %all-to-all-done.1 = bf16[8,18,1024]{2,1,0:T(8,128)(2,1)S(1)} async-done(((bf16[8,18,1024]{2,1,0:T(8,128)(2,1)}), bf16[8,18,1024]{2,1,0:T(8,128)(2,1)S(1)}, u32[]{:S(2)}, u32[]{:S(2)}) %all-to-all-start.1) | async-done | bytes 294944 | tf_op jit(solution)/shard_map/all_to_all | solution.py:50
  329.4 15.3 %reduce-scatter.9.cloned.1.call-done = f32[128,512]{1,0:T(8,128)} async-done(((f32[1024,512]{1,0:T(8,128)}), f32[128,512]{1,0:T(8,128)}) %reduce-scatter.9.cloned.1.call-update) | async-done | bytes 262160 | tf_op jit(solution)/shard_map/reduce_scatter | solution.py:75
  344.6 41.0 %reduce-scatter.11.cloned.1.call-done = f32[128,512]{1,0:T(8,128)} async-done(((f32[1024,512]{1,0:T(8,128)}), f32[128,512]{1,0:T(8,128)}) %reduce-scatter.11.cloned.1.call-update) | async-done | bytes 262160 | tf_op jit(solution)/shard_map/reduce_scatter | solution.py:64
  (35 shorter events, 13.9 us)
Async XLA Ops:
  7.2 124.2 %copy-start = (bf16[1024,512]{1,0:T(8,128)(2,1)S(1)}, bf16[1024,512]{1,0:T(8,128)(2,1)}, u32[]{:S(2)}) copy-start(bf16[1024,512]{1,0:T(8,128)(2,1)} %param.10) | copy-start | bytes 3145732
  7.2 69.6 %all-gather.5.cloned.1.call-start = ((), (), s32[]{:S(2)}) async-start(), calls=%async_computation.10 | async-start | bytes 2654208 | tf_op jit(solution)/shard_map/all_gather | solution.py:43
  31.2 91.1 %all-gather.3.cloned.1.call-start = ((), (), s32[]{:S(2)}) async-start(), calls=%async_computation.8 | async-start | bytes 2654208 | tf_op jit(solution)/shard_map/all_gather | solution.py:43
  49.5 175.3 %reduce-scatter.7.cloned.1.call-start = ((), (), s32[]{:S(2)}) async-start(), calls=%async_computation.11 | async-start | bytes 7077888 | tf_op jit(solution)/shard_map/reduce_scatter | solution.py:48
  131.4 4.4 %copy-start.2 = (bf16[1024,512]{1,0:T(8,128)(2,1)S(1)}, bf16[1024,512]{1,0:T(8,128)(2,1)}, u32[]{:S(2)}) copy-start(bf16[1024,512]{1,0:T(8,128)(2,1)} %param.11) | copy-start | bytes 3145732
  137.8 1.0 copy-start.3
  148.1 156.1 %reduce-scatter.5.cloned.1.call-start = ((), (), s32[]{:S(2)}) async-start(), calls=%async_computation.9 | async-start | bytes 7077888 | tf_op jit(solution)/shard_map/reduce_scatter | solution.py:48
  158.8 185.8 %reduce-scatter.9.cloned.1.call-start = ((), (), s32[]{:S(2)}) async-start(), calls=%async_computation.12 | async-start | bytes 2359296 | tf_op jit(solution)/shard_map/reduce_scatter | solution.py:75
  164.1 221.5 %reduce-scatter.11.cloned.1.call-start = ((), (), s32[]{:S(2)}) async-start(), calls=%async_computation.13 | async-start | bytes 2359296 | tf_op jit(solution)/shard_map/reduce_scatter | solution.py:64
  168.5 144.9 %copy-start.1 = (s32[128]{0:T(128)S(1)}, s32[128]{0:T(128)}, u32[]{:S(2)}) copy-start(s32[128]{0:T(128)} %param.9) | copy-start | bytes 1540
  226.7 79.4 %all-to-all-start.3 = ((bf16[8,18,1024]{2,1,0:T(8,128)(2,1)}), bf16[8,18,1024]{2,1,0:T(8,128)(2,1)S(1)}, u32[]{:S(2)}, u32[]{:S(2)}) async-start(bf16[8,18,1024]{2,1,0:T(8,128)(2,1)} %convert_element_type.25), calls=%async_computation.5 | async-start | bytes 786432 | tf_op jit(solution)/shard_map/all_to_all | solution.py:50
  306.1 20.6 %all-to-all-start.1 = ((bf16[8,18,1024]{2,1,0:T(8,128)(2,1)}), bf16[8,18,1024]{2,1,0:T(8,128)(2,1)S(1)}, u32[]{:S(2)}, u32[]{:S(2)}) async-start(bf16[8,18,1024]{2,1,0:T(8,128)(2,1)} %convert_element_type.22), calls=%async_computation.2 | async-start | bytes 786432 | tf_op jit(solution)/shard_map/all_to_all | solution.py:50
Sparse Core Ops, SparseCore 0:
  31.3 45.4 all-gather.4
  78.9 43.4 all-gather.2
  148.2 76.5 reduce-scatter.6
  227.5 76.6 reduce-scatter.4
  307.4 37.1 reduce-scatter.8
  347.9 37.6 reduce-scatter.10
where the time goes:
time: 393 us; the launch traced here: 392 us
  waiting for transfers between devices  259 us (66%)
  local copies, waits for them, and re-layouts  37.6 us (10%)
  blocking collectives  36.2 us (9%)
  matrix products  24.5 us (6%)
  starting transfers between devices  15 us (4%)
  between operations  14.2 us (4%)
  other arithmetic  5.53 us (1%)
    reduce_scatter x2, waiting for transfers between devices, give_back(): summed = lax.psum_scatter(parts, 'lz', scatter_dimension=0, tiled=True)  126 us
    all_gather x2, waiting for transfers between devices, dispatch(): every = lax.all_gather(by_y, 'lz', axis=0, tiled=True)  65.2 us
    reduce_scatter x1, waiting for transfers between devices, per_device(): lax.psum_scatter(lax.dot_general(flat_grads, hidden_flat, (((0,), (0,)),...  41 us
    all_to_all x2, blocking collectives, dispatch(): lax.all_to_all(place(values), 'ly', split_axis=0, concat_axis=0, tiled=True)  36.2 us
    reduce_scatter x1, waiting for transfers between devices, per_device(): lax.psum_scatter(lax.dot_general(flat_tokens, d_pre, (((0,), (0,)), ((),...  15.3 us
    all_to_all x2, starting transfers between devices, give_back(): return lax.all_to_all(summed, 'ly', split_axis=0, concat_axis=0, tiled=True)  14.6 us
    all_to_all x2, waiting for transfers between devices, give_back(): return lax.all_to_all(summed, 'ly', split_axis=0, concat_axis=0, tiled=True)  11.5 us
    reshape x2, local copies, waits for them, and re-layouts, give_back(): parts = rows.astype(jnp.float32).reshape(-1, capacity, feature_width)  11.2 us
  transfers between devices with their start and end apart: 8, of which 7 were waited for; matrix products, arithmetic and copies ran while one was open for 10% of the time, Pallas kernels for 0%

commit v1 on v0

--- a/solution.py
+++ b/solution.py
@@ -40,7 +40,9 @@
 
     def dispatch(values):
         by_y = lax.all_to_all(place(values), "ly", split_axis=0, concat_axis=0, tiled=True)
-        every = lax.all_gather(by_y, "lz", axis=0, tiled=True)
+        every = jnp.concatenate(
+            lax.all_to_all(jnp.stack([by_y] * lax.axis_size("lz")), "lz", 0, 0), axis=0
+        )
         return every.reshape(-1, feature_width)
 
     def give_back(rows):

time: 393 us -> 447 us (1.14)
  waiting for transfers between devices: 259 us -> 313 us
  blocking collectives: 36.2 us -> 0 us
  starting transfers between devices: 15 us -> 46.3 us
  local copies, waits for them, and re-layouts: 37.6 us -> 42.4 us
    all_to_all x0 -> x4, waiting for transfers between devices: none -> 117 us  [the longest x2 98.5 us: dispatch(): lax.all_to_all(jnp.stack([by_y] * lax.axis_size('lz')), 'lz', 0, 0)]
    all_gather x2 -> x0, waiting for transfers between devices: 65.2 us -> none  [dispatch(): every = lax.all_gather(by_y, 'lz', axis=0, tiled=True)]
    all_to_all x2 -> x0, blocking collectives: 36.2 us -> none  [dispatch(): lax.all_to_all(place(values), 'ly', split_axis=0, concat_axis=0, tiled=True)]
    all_to_all x0 -> x4, starting transfers between devices: none -> 31.5 us  [the longest x2 17.5 us: dispatch(): lax.all_to_all(jnp.stack([by_y] * lax.axis_size('lz')), 'lz', 0, 0)]
    another operation x0 -> x4, local copies, waits for them, and re-layouts: none -> 11.6 us  [the longest x2 7.26 us: dispatch(): return every.reshape(-1, feature_width)]
    all_gather x2 -> x0, local copies, waits for them, and re-layouts: 9.35 us -> none  [dispatch(): every = lax.all_gather(by_y, 'lz', axis=0, tiled=True)]
    all_to_all x0 -> x2, local copies, waits for them, and re-layouts: none -> 8.01 us  [dispatch(): lax.all_to_all(jnp.stack([by_y] * lax.axis_size('lz')), 'lz', 0, 0)]
    reshape x2 -> x0, local copies, waits for them, and re-layouts: 7.28 us -> none  [dispatch(): return every.reshape(-1, feature_width)]
  transfers between devices with their start and end apart: 8 -> 10, of which waited for: 7 -> 9; matrix products, arithmetic and copies ran while one was open for 10% -> 9% of each run, Pallas kernels for 0% -> 0%
where the time goes in v1:
time: 447 us; the launch traced here: 445 us
  waiting for transfers between devices  313 us (70%)
  starting transfers between devices  46.3 us (10%)
  local copies, waits for them, and re-layouts  42.4 us (9%)
  matrix products  24.2 us (5%)
  between operations  13.9 us (3%)
  other arithmetic  5.57 us (1%)
    reduce_scatter x2, waiting for transfers between devices, give_back(): summed = lax.psum_scatter(parts, 'lz', scatter_dimension=0, tiled=True)  127 us
    all_to_all x2, waiting for transfers between devices, dispatch(): lax.all_to_all(jnp.stack([by_y] * lax.axis_size('lz')), 'lz', 0, 0)  98.5 us
    reduce_scatter x1, waiting for transfers between devices, per_device(): lax.psum_scatter(lax.dot_general(flat_grads, hidden_flat, (((0,), (0,)),...  40.9 us
    all_to_all x2, waiting for transfers between devices, dispatch(): lax.all_to_all(place(values), 'ly', split_axis=0, concat_axis=0, tiled=True)  18.9 us
    all_to_all x2, starting transfers between devices, dispatch(): lax.all_to_all(jnp.stack([by_y] * lax.axis_size('lz')), 'lz', 0, 0)  17.5 us
    reduce_scatter x1, waiting for transfers between devices, per_device(): lax.psum_scatter(lax.dot_general(flat_tokens, d_pre, (((0,), (0,)), ((),...  15.5 us
    all_to_all x2, starting transfers between devices, give_back(): return lax.all_to_all(summed, 'ly', split_axis=0, concat_axis=0, tiled=True)  14.5 us
    all_to_all x2, starting transfers between devices, dispatch(): lax.all_to_all(place(values), 'ly', split_axis=0, concat_axis=0, tiled=True)  14 us
  transfers between devices with their start and end apart: 10, of which 9 were waited for; matrix products, arithmetic and copies ran while one was open for 9% of the time, Pallas kernels for 0%

profile of v1, /device:TPU:8, one launch (start us, length us, event | category | flops | bytes accessed | tf_op | source)
XLA Modules:
  0.0 445.3 jit_solution(15348253458804898525)
XLA Ops:
  10.4 9.2 %all-to-all-start.3 = ((bf16[8,18,1024]{2,1,0:T(8,128)(2,1)}), bf16[8,18,1024]{2,1,0:T(8,128)(2,1)S(1)}, u32[]{:S(2)}, u32[]{:S(2)}) async-start(bf16[8,18,1024]{2,1,0:T(8,128)(2,1)} %reshape.34), calls=%async_computation.4 | async-start | bytes 786432 | tf_op jit(solution)/shard_map/all_to_all | solution.py:42
  22.1 9.1 %all-to-all-done.3 = bf16[8,18,1024]{2,1,0:T(8,128)(2,1)S(1)} async-done(((bf16[8,18,1024]{2,1,0:T(8,128)(2,1)}), bf16[8,18,1024]{2,1,0:T(8,128)(2,1)S(1)}, u32[]{:S(2)}, u32[]{:S(2)}) %all-to-all-start.3) | async-done | bytes 294944 | tf_op jit(solution)/shard_map/all_to_all | solution.py:42
  31.2 4.8 %all-to-all-start = ((bf16[8,18,1024]{2,1,0:T(8,128)(2,1)}), bf16[8,18,1024]{2,1,0:T(8,128)(2,1)S(1)}, u32[]{:S(2)}, u32[]{:S(2)}) async-start(bf16[8,18,1024]{2,1,0:T(8,128)(2,1)} %reshape.31), calls=%async_computation | async-start | bytes 786432 | tf_op jit(solution)/shard_map/all_to_all | solution.py:42
  36.2 9.8 %all-to-all-done = bf16[8,18,1024]{2,1,0:T(8,128)(2,1)S(1)} async-done(((bf16[8,18,1024]{2,1,0:T(8,128)(2,1)}), bf16[8,18,1024]{2,1,0:T(8,128)(2,1)S(1)}, u32[]{:S(2)}, u32[]{:S(2)}) %all-to-all-start) | async-done | bytes 294944 | tf_op jit(solution)/shard_map/all_to_all | solution.py:42
  47.8 13.1 %all-to-all-start.4 = ((bf16[8,8,18,1024]{3,1,2,0:T(8,128)(2,1)}), bf16[8,8,18,1024]{3,1,2,0:T(8,128)(2,1)S(1)}, u32[]{:S(2)}, u32[]{:S(2)}) async-start(bf16[8,8,18,1024]{3,1,2,0:T(8,128)(2,1)} %stack.5), calls=%async_computation.5 | async-start | bytes 4718592 | tf_op jit(solution)/shard_map/all_to_all | solution.py:44
  62.7 51.5 %all-to-all-done.4 = bf16[8,8,18,1024]{3,1,2,0:T(8,128)(2,1)S(1)} async-done(((bf16[8,8,18,1024]{3,1,2,0:T(8,128)(2,1)}), bf16[8,8,18,1024]{3,1,2,0:T(8,128)(2,1)S(1)}, u32[]{:S(2)}, u32[]{:S(2)}) %all-to-all-start.4) | async-done | bytes 2359328 | tf_op jit(solution)/shard_map/all_to_all | solution.py:44
  116.8 4.4 all-to-all-start.1
  127.4 47.1 %all-to-all-done.1 = bf16[8,8,18,1024]{3,1,2,0:T(8,128)(2,1)} async-done(((bf16[8,8,18,1024]{3,1,2,0:T(8,128)(2,1)}), bf16[8,8,18,1024]{3,1,2,0:T(8,128)(2,1)}, u32[]{:S(2)}, u32[]{:S(2)}) %all-to-all-start.1) | async-done | bytes 2359328 | tf_op jit(solution)/shard_map/all_to_all | solution.py:44
  174.4 4.8 %copy.15 = bf16[8,8,18,1024]{3,2,1,0:T(8,128)(2,1)} copy(bf16[8,8,18,1024]{3,1,2,0:T(8,128)(2,1)} %all-to-all-done.1) | data formatting | bytes 4718592 | tf_op jit(solution)/shard_map/all_to_all | solution.py:44
  179.3 4.3 reshape_reshape.6
  183.6 4.4 multiply_convert_fusion
  191.1 3.6 fusion.1
  194.7 5.6 %reshape.40 = f32[64,18,1024]{2,1,0:T(8,128)} reshape(f32[1152,1024]{1,0:T(8,128)} %fusion.1) | data formatting | bytes 9437184 | tf_op jit(solution)/shard_map/reshape | solution.py:49
  200.4 5.1 %fusion = f32[1152,1024]{1,0:T(8,128)} fusion(bf16[1152,512]{1,0:T(8,128)(2,1)} %get-tuple-element.8, bf16[1024,512]{1,0:T(8,128)(2,1)} %param.11), kind=kOutput, calls=%fused_computation.6 | convolution fusion | flops 1210318848 | bytes 6946816 | tf_op jit(solution)/shard_map/dot_general | solution.py:62
  205.5 5.6 %reshape.38 = f32[64,18,1024]{2,1,0:T(8,128)} reshape(f32[1152,1024]{1,0:T(8,128)} %fusion) | data formatting | bytes 9437184 | tf_op jit(solution)/shard_map/reshape | solution.py:49
  211.3 4.9 %convolution_multiply_fusion.2 = f32[1024,512]{1,0:T(8,128)} fusion(bf16[1152,1024]{1,0:T(8,128)(2,1)} %reshape_reshape.6, bf16[1152,512]{1,0:T(8,128)(2,1)} %copy-done.4), kind=kOutput, calls=%fused_computation.18 | convolution fusion | flops 1208483840 | bytes 5636096 | tf_op jit(solution)/shard_map/dot_general | solution.py:78
  216.3 4.1 convolution_multiply_fusion.1
  220.5 57.2 %reduce-scatter.7.cloned.1.call-done = f32[8,18,1024]{2,1,0:T(8,128)} async-done(((f32[64,18,1024]{2,1,0:T(8,128)}), f32[8,18,1024]{2,1,0:T(8,128)}) %reduce-scatter.7.cloned.1.call-update) | async-done | bytes 589840 | tf_op jit(solution)/shard_map/reduce_scatter | solution.py:50
  279.6 7.3 %all-to-all-start.5 = ((bf16[8,18,1024]{2,1,0:T(8,128)(2,1)}), bf16[8,18,1024]{2,1,0:T(8,128)(2,1)S(1)}, u32[]{:S(2)}, u32[]{:S(2)}) async-start(bf16[8,18,1024]{2,1,0:T(8,128)(2,1)} %convert_element_type.25), calls=%async_computation.7 | async-start | bytes 786432 | tf_op jit(solution)/shard_map/all_to_all | solution.py:52
  286.9 70.3 %reduce-scatter.5.cloned.1.call-done = f32[8,18,1024]{2,1,0:T(8,128)} async-done(((f32[64,18,1024]{2,1,0:T(8,128)}), f32[8,18,1024]{2,1,0:T(8,128)}) %reduce-scatter.5.cloned.1.call-update) | async-done | bytes 589840 | tf_op jit(solution)/shard_map/reduce_scatter | solution.py:50
  359.1 7.3 %all-to-all-start.2 = ((bf16[8,18,1024]{2,1,0:T(8,128)(2,1)}), bf16[8,18,1024]{2,1,0:T(8,128)(2,1)S(1)}, u32[]{:S(2)}, u32[]{:S(2)}) async-start(bf16[8,18,1024]{2,1,0:T(8,128)(2,1)} %convert_element_type.22), calls=%async_computation.3 | async-start | bytes 786432 | tf_op jit(solution)/shard_map/all_to_all | solution.py:52
  368.2 11.5 %all-to-all-done.2 = bf16[8,18,1024]{2,1,0:T(8,128)(2,1)S(1)} async-done(((bf16[8,18,1024]{2,1,0:T(8,128)(2,1)}), bf16[8,18,1024]{2,1,0:T(8,128)(2,1)S(1)}, u32[]{:S(2)}, u32[]{:S(2)}) %all-to-all-start.2) | async-done | bytes 294944 | tf_op jit(solution)/shard_map/all_to_all | solution.py:52
  382.4 15.5 %reduce-scatter.9.cloned.1.call-done = f32[128,512]{1,0:T(8,128)} async-done(((f32[1024,512]{1,0:T(8,128)}), f32[128,512]{1,0:T(8,128)}) %reduce-scatter.9.cloned.1.call-update) | async-done | bytes 262160 | tf_op jit(solution)/shard_map/reduce_scatter | solution.py:77
  397.9 40.9 %reduce-scatter.11.cloned.1.call-done = f32[128,512]{1,0:T(8,128)} async-done(((f32[1024,512]{1,0:T(8,128)}), f32[128,512]{1,0:T(8,128)}) %reduce-scatter.11.cloned.1.call-update) | async-done | bytes 262160 | tf_op jit(solution)/shard_map/reduce_scatter | solution.py:66
  (39 shorter events, 30.1 us)
Async XLA Ops:
  7.2 176.5 %copy-start = (bf16[1024,512]{1,0:T(8,128)(2,1)S(1)}, bf16[1024,512]{1,0:T(8,128)(2,1)}, u32[]{:S(2)}) copy-start(bf16[1024,512]{1,0:T(8,128)(2,1)} %param.10) | copy-start | bytes 3145732
  10.4 20.8 %all-to-all-start.3 = ((bf16[8,18,1024]{2,1,0:T(8,128)(2,1)}), bf16[8,18,1024]{2,1,0:T(8,128)(2,1)S(1)}, u32[]{:S(2)}, u32[]{:S(2)}) async-start(bf16[8,18,1024]{2,1,0:T(8,128)(2,1)} %reshape.34), calls=%async_computation.4 | async-start | bytes 786432 | tf_op jit(solution)/shard_map/all_to_all | solution.py:42
  31.2 14.8 %all-to-all-start = ((bf16[8,18,1024]{2,1,0:T(8,128)(2,1)}), bf16[8,18,1024]{2,1,0:T(8,128)(2,1)S(1)}, u32[]{:S(2)}, u32[]{:S(2)}) async-start(bf16[8,18,1024]{2,1,0:T(8,128)(2,1)} %reshape.31), calls=%async_computation | async-start | bytes 786432 | tf_op jit(solution)/shard_map/all_to_all | solution.py:42
  46.0 1.7 copy-start.1
  47.8 66.4 %all-to-all-start.4 = ((bf16[8,8,18,1024]{3,1,2,0:T(8,128)(2,1)}), bf16[8,8,18,1024]{3,1,2,0:T(8,128)(2,1)S(1)}, u32[]{:S(2)}, u32[]{:S(2)}) async-start(bf16[8,8,18,1024]{3,1,2,0:T(8,128)(2,1)} %stack.5), calls=%async_computation.5 | async-start | bytes 4718592 | tf_op jit(solution)/shard_map/all_to_all | solution.py:44
  116.8 57.6 %all-to-all-start.1 = ((bf16[8,8,18,1024]{3,1,2,0:T(8,128)(2,1)}), bf16[8,8,18,1024]{3,1,2,0:T(8,128)(2,1)}, u32[]{:S(2)}, u32[]{:S(2)}) async-start(bf16[8,8,18,1024]{3,1,2,0:T(8,128)(2,1)} %stack.4), calls=%async_computation.1 | async-start | bytes 4718592 | tf_op jit(solution)/shard_map/all_to_all | solution.py:44
  121.2 156.4 %reduce-scatter.7.cloned.1.call-start = ((), (), s32[]{:S(2)}) async-start(), calls=%async_computation.11 | async-start | bytes 7077888 | tf_op jit(solution)/shard_map/reduce_scatter | solution.py:50
  183.6 4.4 copy-start.3
  190.0 1.0 copy-start.4
  200.3 156.9 %reduce-scatter.5.cloned.1.call-start = ((), (), s32[]{:S(2)}) async-start(), calls=%async_computation.10 | async-start | bytes 7077888 | tf_op jit(solution)/shard_map/reduce_scatter | solution.py:50
  211.1 186.8 %reduce-scatter.9.cloned.1.call-start = ((), (), s32[]{:S(2)}) async-start(), calls=%async_computation.12 | async-start | bytes 2359296 | tf_op jit(solution)/shard_map/reduce_scatter | solution.py:77
  216.3 222.5 %reduce-scatter.11.cloned.1.call-start = ((), (), s32[]{:S(2)}) async-start(), calls=%async_computation.13 | async-start | bytes 2359296 | tf_op jit(solution)/shard_map/reduce_scatter | solution.py:66
  220.5 145.9 %copy-start.2 = (s32[128]{0:T(128)S(1)}, s32[128]{0:T(128)}, u32[]{:S(2)}) copy-start(s32[128]{0:T(128)} %param.9) | copy-start | bytes 1540
  279.6 79.5 %all-to-all-start.5 = ((bf16[8,18,1024]{2,1,0:T(8,128)(2,1)}), bf16[8,18,1024]{2,1,0:T(8,128)(2,1)S(1)}, u32[]{:S(2)}, u32[]{:S(2)}) async-start(bf16[8,18,1024]{2,1,0:T(8,128)(2,1)} %convert_element_type.25), calls=%async_computation.7 | async-start | bytes 786432 | tf_op jit(solution)/shard_map/all_to_all | solution.py:52
  359.1 20.6 %all-to-all-start.2 = ((bf16[8,18,1024]{2,1,0:T(8,128)(2,1)}), bf16[8,18,1024]{2,1,0:T(8,128)(2,1)S(1)}, u32[]{:S(2)}, u32[]{:S(2)}) async-start(bf16[8,18,1024]{2,1,0:T(8,128)(2,1)} %convert_element_type.22), calls=%async_computation.3 | async-start | bytes 786432 | tf_op jit(solution)/shard_map/all_to_all | solution.py:52
Sparse Core Ops, SparseCore 0:
  200.5 77.1 reduce-scatter.6
  280.5 76.6 reduce-scatter.4
  360.6 37.1 reduce-scatter.8
  401.1 37.6 reduce-scatter.10
